TPU v7x, 256 devices: a whole 4x4x8 slice. The times are simulated.
256 devices in a mesh: ia: 4 (over y), ja: 4 (over x), ka: 16 (over z, core).
Axes of the slice: x: 4, y: 4, z: 8, core: 2. Of those that a mesh axis runs over, the one named last changes fastest.
Arguments:
- blocks: bfloat16 [4, 4, 16, 2, 128, 128, 128], P('ia', 'ja', 'ka'), may hold values from -6 to 6
- first_mode_rows: int32 [4, 4, 16, 2], P('ia', 'ja', 'ka'), may hold values from 0 to 15
- second_mode_rows: int32 [4, 4, 16, 2], P('ia', 'ja', 'ka'), may hold values from 0 to 15
- third_mode_rows: int32 [4, 4, 16, 2], P('ia', 'ja', 'ka'), may hold values from 0 to 3
- filled: int32 [4, 4, 16], P('ia', 'ja', 'ka'), may hold values from 1 to 2, as said below
- owner_one: int32 [64], replicated, may hold values from 0 to 63, each once
- owner_two: int32 [64], replicated, may hold values from 0 to 63, each once
- factor_b: float32 [4, 2048, 256], P('ja', ('ia', 'ka'))
- factor_c: float32 [16, 512, 256], P('ka')
Outputs:
- a_new: float32 [4, 2048, 256], P('ia', ('ja', 'ka'))
- b_new: float32 [4, 2048, 256], P('ja', ('ia', 'ka'))
Inputs may be any that keep to these rules, and one draw needn't show every extreme that they name: Number of nonempty slots of a grid cell; at least one cell has all 2 slots filled. Slots at or beyond this count hold data that is not part of the tensor.
All inputs are finite; a program needn't handle non-finite values.
Results may differ from a plain program's by a relative error of at most 0.0039.
The roundings to bfloat16 on the way count: a program that leaves them out, or rounds other values in their place, can miss the bound.
Values may be sent and summed in bfloat16 or wider, within the bound.
A program may use at most 128 MiB of HBM per device.

v0:
```python
import jax
import jax.numpy as jnp
from jax import lax
from jax.sharding import PartitionSpec as P

EPS = 1e-06


def solve_rows(gram, rows):
    lower = jnp.linalg.cholesky(gram)
    return jax.scipy.linalg.cho_solve((lower, True), rows.T).T


def add_rows(accum, start, contrib):
    current = lax.dynamic_slice_in_dim(accum, start, contrib.shape[0], 0)
    return lax.dynamic_update_slice_in_dim(accum, current + contrib, start, 0)


def batched_sum(inner, weights):
    summed = lax.dot_general(
        inner,
        weights.astype(jnp.float32),
        (((1,), (0,)), ((2,), (1,))),
        precision=lax.Precision.HIGHEST,
        preferred_element_type=jnp.float32,
    )
    return summed.T


def to_logical(stored, owner, piece_rows):
    return stored.reshape(-1, piece_rows, stored.shape[1])[owner].reshape(stored.shape)


def to_stored(logical, owner, piece_rows):
    positions = jnp.arange(owner.shape[0], dtype=jnp.int32)
    inverse = jnp.sum(
        jnp.where(owner[None, :] == positions[:, None], positions[None, :], 0), axis=1
    )
    return logical.reshape(-1, piece_rows, logical.shape[1])[inverse].reshape(logical.shape)


def keep_same(value):
    return value


def partial_value(function, slot):

    def applied(value):
        return function(value, slot)

    return applied


def body(
    blocks,
    first_mode_rows,
    second_mode_rows,
    third_mode_rows,
    filled,
    owner_one,
    owner_two,
    factor_b,
    factor_c,
):
    highest = lax.Precision.HIGHEST
    piece_rows = factor_b.shape[1]
    rank_width = factor_b.shape[2]
    block_edge = blocks.shape[-1]
    slot_count = blocks.shape[3]
    total_one = piece_rows * lax.axis_size("ia") * lax.axis_size("ja") * lax.axis_size("ka")
    slab_rows_one = piece_rows * lax.axis_size("ja") * lax.axis_size("ka")
    slab_rows_two = piece_rows * lax.axis_size("ia") * lax.axis_size("ka")
    own_b = factor_b[0]
    own_c = lax.dynamic_slice_in_dim(
        factor_c[0], lax.axis_index(("ia", "ja")) * piece_rows, piece_rows, 0
    )
    local_b = jnp.dot(own_b.T, own_b, precision=highest, preferred_element_type=jnp.float32)
    local_c = jnp.dot(own_c.T, own_c, precision=highest, preferred_element_type=jnp.float32)
    gram_b, gram_c = lax.psum((local_b, local_c), ("ia", "ja", "ka"))
    stored_b = lax.all_gather(factor_b.astype(jnp.bfloat16), ("ia", "ka"), axis=1, tiled=True)[0]
    half_b = to_logical(stored_b, owner_two, piece_rows)
    half_c = factor_c[0].astype(jnp.bfloat16)
    live_count = filled[0, 0, 0]

    def update_one(partial_sum, slot):
        block = blocks[0, 0, 0, slot]
        b_rows = lax.dynamic_slice_in_dim(
            half_b, second_mode_rows[0, 0, 0, slot] * block_edge, block_edge, 0
        )
        c_rows = lax.dynamic_slice_in_dim(
            half_c, third_mode_rows[0, 0, 0, slot] * block_edge, block_edge, 0
        )
        inner = jnp.dot(
            block.reshape(block_edge * block_edge, block_edge),
            c_rows,
            preferred_element_type=jnp.float32,
        )
        inner = inner.reshape(block_edge, block_edge, rank_width)
        contrib = batched_sum(inner, b_rows)
        return add_rows(partial_sum, first_mode_rows[0, 0, 0, slot] * block_edge, contrib)

    partial_one = jnp.zeros((slab_rows_one, rank_width), jnp.float32)
    for slot in range(slot_count):
        partial_one = lax.cond(
            slot < live_count, partial_value(update_one, slot), keep_same, partial_one
        )
    stored_one = to_stored(partial_one, owner_one, piece_rows)
    system_one = gram_b * gram_c
    summed_own = lax.psum_scatter(stored_one, ("ja", "ka"), scatter_dimension=0, tiled=True)
    a_hat = solve_rows(system_one, summed_own)
    squares_a = lax.psum(jnp.sum(a_hat * a_hat, axis=0), ("ia", "ja", "ka"))
    scale_a = jnp.sqrt(squares_a / total_one + EPS)
    a_own = a_hat / scale_a
    local_a = jnp.dot(a_own.T, a_own, precision=highest, preferred_element_type=jnp.float32)
    gram_a = lax.psum(local_a, ("ia", "ja", "ka"))
    stored_a = lax.all_gather(a_own.astype(jnp.bfloat16)[None], ("ja", "ka"), axis=1, tiled=True)[0]
    half_a = to_logical(stored_a, owner_one, piece_rows)

    def update_two(partial_sum, slot):
        block = blocks[0, 0, 0, slot]
        a_rows = lax.dynamic_slice_in_dim(
            half_a, first_mode_rows[0, 0, 0, slot] * block_edge, block_edge, 0
        )
        c_rows = lax.dynamic_slice_in_dim(
            half_c, third_mode_rows[0, 0, 0, slot] * block_edge, block_edge, 0
        )
        inner = lax.dot_general(
            block.reshape(block_edge, block_edge * block_edge),
            a_rows,
            (((0,), (0,)), ((), ())),
            preferred_element_type=jnp.float32,
        )
        inner = inner.reshape(block_edge, block_edge, rank_width)
        contrib = batched_sum(inner, c_rows)
        return add_rows(partial_sum, second_mode_rows[0, 0, 0, slot] * block_edge, contrib)

    partial_two = jnp.zeros((slab_rows_two, rank_width), jnp.float32)
    for slot in range(slot_count):
        partial_two = lax.cond(
            slot < live_count, partial_value(update_two, slot), keep_same, partial_two
        )
    stored_two = to_stored(partial_two, owner_two, piece_rows)
    summed_two = lax.psum_scatter(stored_two, ("ia", "ka"), scatter_dimension=0, tiled=True)
    b_hat = solve_rows(gram_a * gram_c, summed_two)
    squares_b = lax.psum(jnp.sum(b_hat * b_hat, axis=0), ("ia", "ja", "ka"))
    b_own = b_hat / jnp.sqrt(squares_b / total_one + EPS)
    return (a_own[None], b_own[None])


def solution(mesh):
    return jax.shard_map(
        body,
        mesh=mesh,
        in_specs=(
            P("ia", "ja", "ka", None, None, None, None),
            P("ia", "ja", "ka", None),
            P("ia", "ja", "ka", None),
            P("ia", "ja", "ka", None),
            P("ia", "ja", "ka"),
            P(),
            P(),
            P("ja", ("ia", "ka"), None),
            P("ka", None, None),
        ),
        out_specs=(P("ia", ("ja", "ka"), None), P("ja", ("ia", "ka"), None)),
        check_vma=False,
    )
```

profile of v0, /device:TPU:1, one launch (start us, length us, event | category | flops | bytes accessed | tf_op | source)
XLA Modules:
  0.0 827.5 jit_solution(4852424667202017735)
XLA Ops:
  9.5 2.0 fusion.34
  11.5 2.0 fusion.36
  17.5 75.5 %all-gather.4.cloned.1.call-done = bf16[1,2048,256]{2,1,0:T(8,128)(2,1)} async-done(((bf16[1,32,256]{2,1,0:T(8,128)(2,1)}), bf16[1,2048,256]{2,1,0:T(8,128)(2,1)}) %all-gather.4.cloned.1.call-update) | async-done | bytes 1048592 | tf_op jit(solution)/shard_map/all_gather | solution.py:80
  93.0 1.8 gather_fusion
  94.8 23.3 %conditional.4 = (f32[2048,256]{1,0:T(8,128)}) conditional(s32[]{:T(128)} %bitcast.41, () %tuple.54, (s32[1,1,1,2]{3,2,1,0:T(1,128)}, bf16[512,256]{1,0:T(8,128)(2,1)S(1)}, bf16[1,1,1,2,128,128,128]{6,5,4,3,2,1,0:T(8,128)(2,1)}, s32[1,1,1,2]{3,2,1,0:T(1,128)}, bf16[2048,256]{1,0:T(8,128)(2,1)S(1)}, /*index=5*/s32[1,1,1,2]{3,2,1,0:T(1,128)}) %tuple.134), branch_computations={%region_6.0_spmd, %region_7.0_spmd} | conditional | flops 1082130432 | bytes 83099928 | solution.py:104
  95.5 2.8 slice.76
  98.3 2.4 convolution_bitcast_fusion
  100.7 6.7 copy.52
  107.6 8.2 multiply_reduce_fusion
  118.1 3.6 gather_fusion.1
  122.1 149.6 %all-reduce.7.cloned.1.call-done = (f32[256,256]{0,1:T(8,128)}, f32[256,256]{0,1:T(8,128)}) async-done(((f32[256,256]{0,1:T(8,128)}, f32[256,256]{0,1:T(8,128)}), (f32[256,256]{0,1:T(8,128)}, f32[256,256]{0,1:T(8,128)})) %all-reduce.7.cloned.1.call-update) | async-done | bytes 524304 | tf_op jit(solution)/shard_map/psum | solution.py:79
  272.9 11.7 %cholesky.130 = f32[128,128]{1,0:T(8,128)S(1)} custom-call(f32[128,128]{1,0:T(8,128)S(1)} %cholesky.194), custom_call_target="Cholesky" | custom-call | tf_op jit(solution)/shard_map/jit(cholesky)/cholesky | solution.py:10
  284.7 9.8 %custom-call.15 = f32[1,128,128]{1,2,0:T(8,128)S(1)} custom-call(f32[1,128,128]{2,1,0:T(8,128)S(1)} %get-tuple-element.155), custom_call_target="InvertDiagBlocksLowerTriangular" | custom-call | tf_op jit(solution)/shard_map/jit(cholesky)/cholesky | solution.py:10
  295.0 11.7 %cholesky.147 = f32[128,128]{1,0:T(8,128)S(1)} custom-call(f32[128,128]{1,0:T(8,128)S(1)} %convolution_subtract_fusion.1), custom_call_target="Cholesky" | custom-call | tf_op jit(solution)/shard_map/jit(cholesky)/cholesky | solution.py:10
  308.8 14.6 %while.4 = (s32[]{:T(128)}, f32[256,256]{1,0:T(8,128)S(1)}, s32[2,2]{1,0:T(2,128)S(1)}, f32[2,128,128]{2,1,0:T(8,128)S(1)}, s32[]{:T(128)}) while((s32[]{:T(128)}, f32[256,256]{1,0:T(8,128)S(1)}, s32[2,2]{1,0:T(2,128)S(1)}, f32[2,128,128]{2,1,0:T(8,128)S(1)}, s32[]{:T(128)}) %tuple.103), condition=%wide.while_cond, body=%wide.while_body.sunk | while | flops 2 | bytes 131181 | solution.py:11
  323.4 19.7 %custom-call.16 = f32[2,128,128]{1,2,0:T(8,128)S(1)} custom-call(f32[2,128,128]{2,1,0:T(8,128)S(1)} %get-tuple-element.124), custom_call_target="InvertDiagBlocksLowerTriangular" | custom-call | tf_op jit(solution)/shard_map/jit(_cho_solve)/triangular_solve | solution.py:11
  345.9 77.9 %psum.37 = f32[256]{0:T(256)S(1)} all-reduce(f32[256]{0:T(256)S(1)} %multiply_reduce_fusion.5), channel_id=1, replica_groups=mesh['ia'=4,'ja'=4,'ka'=16] {'ia','ja','ka'}, use_global_device_ids=true, to_apply=%region_13.16 | all-reduce | flops 256 | bytes 2048 | tf_op jit(solution)/shard_map/psum | solution.py:111
  425.8 71.7 %all-gather.6.cloned.1.call-done = bf16[2048,256]{1,0:T(8,128)(2,1)} async-done(((bf16[32,256]{1,0:T(8,128)(2,1)}), bf16[2048,256]{1,0:T(8,128)(2,1)}) %all-gather.6.cloned.1.call-update) | async-done | bytes 1048592 | tf_op jit(solution)/shard_map/all_gather | solution.py:116
  497.5 1.8 gather_fusion.2
  499.4 23.6 %conditional.6 = (f32[2048,256]{1,0:T(8,128)}) conditional(s32[]{:T(128)} %bitcast.41, () %tuple.57, (s32[1,1,1,2]{3,2,1,0:T(1,128)S(1)}, bf16[2048,256]{1,0:T(8,128)(2,1)S(1)}, bf16[1,1,1,2,128,128,128]{6,5,4,3,2,1,0:T(8,128)(2,1)}, s32[1,1,1,2]{3,2,1,0:T(1,128)S(1)}, bf16[512,256]{1,0:T(8,128)(2,1)S(1)}, ...), branch_computations={%region_15.18_spmd, %region_16.19_spmd} | conditional | flops 1082130432 | bytes 83099800 | solution.py:139
  499.4 2.5 slice.84
  501.9 3.6 convolution_bitcast_fusion.2
  505.5 6.7 copy.55
  512.4 8.3 multiply_reduce_fusion.2
  523.1 3.7 gather_fusion.3
  526.8 150.8 %all-reduce.5.cloned.1.call-done = f32[256,256]{0,1:T(8,128)} async-done(((f32[256,256]{0,1:T(8,128)}), f32[256,256]{0,1:T(8,128)}) %all-reduce.5.cloned.1.call-update) | async-done | bytes 262160 | tf_op jit(solution)/shard_map/psum | solution.py:115
  678.8 11.7 %cholesky.164 = f32[128,128]{1,0:T(8,128)S(1)} custom-call(f32[128,128]{1,0:T(8,128)S(1)} %cholesky.197), custom_call_target="Cholesky" | custom-call | tf_op jit(solution)/shard_map/jit(cholesky)/cholesky | solution.py:10
  690.6 9.8 %custom-call.17 = f32[1,128,128]{1,2,0:T(8,128)S(1)} custom-call(f32[1,128,128]{2,1,0:T(8,128)S(1)} %get-tuple-element.151), custom_call_target="InvertDiagBlocksLowerTriangular" | custom-call | tf_op jit(solution)/shard_map/jit(cholesky)/cholesky | solution.py:10
  700.9 11.7 %cholesky.181 = f32[128,128]{1,0:T(8,128)S(1)} custom-call(f32[128,128]{1,0:T(8,128)S(1)} %convolution_subtract_fusion), custom_call_target="Cholesky" | custom-call | tf_op jit(solution)/shard_map/jit(cholesky)/cholesky | solution.py:10
  715.2 4.2 while.5
  719.4 19.7 %custom-call.18 = f32[2,128,128]{1,2,0:T(8,128)S(1)} custom-call(f32[2,128,128]{2,1,0:T(8,128)S(1)} %get-tuple-element.125), custom_call_target="InvertDiagBlocksLowerTriangular" | custom-call | tf_op jit(solution)/shard_map/jit(_cho_solve)/triangular_solve | solution.py:11
  742.0 77.3 %psum.39 = f32[256]{0:T(256)S(1)} all-reduce(f32[256]{0:T(256)S(1)} %multiply_reduce_fusion.4), channel_id=1, replica_groups=mesh['ia'=4,'ja'=4,'ka'=16] {'ia','ja','ka'}, use_global_device_ids=true, to_apply=%region_22.25 | all-reduce | flops 256 | bytes 2048 | tf_op jit(solution)/shard_map/psum | solution.py:145
  (109 shorter events, 31.6 us)
Async XLA Ops:
  8.0 85.0 %all-gather.4.cloned.1.call-start = ((), (), s32[]{:S(2)}) async-start(), calls=%async_computation.2 | async-start | bytes 1064960 | tf_op jit(solution)/shard_map/all_gather | solution.py:80
  9.4 262.2 %all-reduce.7.cloned.1.call-start = ((), (), s32[]{:S(2)}) async-start(), calls=%async_computation.7 | async-start | bytes 1048576 | tf_op jit(solution)/shard_map/psum | solution.py:79
  13.5 329.6 %reduce-scatter.3.cloned.1.call-start = ((), (), s32[]{:S(2)}) async-start(), calls=%async_computation.3 | async-start | bytes 2129920 | tf_op jit(solution)/shard_map/reduce_scatter | solution.py:109
  100.7 6.7 copy-start.4
  107.5 8.4 %copy-start.7 = (s32[1,1,1,2]{3,2,1,0:T(1,128)S(1)}, s32[1,1,1,2]{3,2,1,0:T(1,128)}, u32[]{:S(2)}) copy-start(s32[1,1,1,2]{3,2,1,0:T(1,128)} %get-tuple-element.85) | copy-start | bytes 28 | tf_op jit(solution)/shard_map/cond
  121.7 302.8 %copy-start.1 = (s32[64]{0:T(128)S(1)}, s32[64]{0:T(128)}, u32[]{:S(2)}) copy-start(s32[64]{0:T(128)} %param.25) | copy-start | bytes 772
  121.8 375.7 %all-gather.6.cloned.1.call-start = ((), (), s32[]{:S(2)}) async-start(), calls=%async_computation.6 | async-start | bytes 1064960 | tf_op jit(solution)/shard_map/all_gather | solution.py:116
  271.6 227.7 %copy-start.2 = (s32[1,1,1,2]{3,2,1,0:T(1,128)S(1)}, s32[1,1,1,2]{3,2,1,0:T(1,128)}, u32[]{:S(2)}) copy-start(s32[1,1,1,2]{3,2,1,0:T(1,128)} %param.23) | copy-start | bytes 28
  271.6 227.7 %copy-start.3 = (s32[1,1,1,2]{3,2,1,0:T(1,128)S(1)}, s32[1,1,1,2]{3,2,1,0:T(1,128)}, u32[]{:S(2)}) copy-start(s32[1,1,1,2]{3,2,1,0:T(1,128)} %param.22) | copy-start | bytes 28
  271.6 227.7 %copy-start.6 = (s32[1,1,1,2]{3,2,1,0:T(1,128)S(1)}, s32[1,1,1,2]{3,2,1,0:T(1,128)}, u32[]{:S(2)}) copy-start(s32[1,1,1,2]{3,2,1,0:T(1,128)} %param.21) | copy-start | bytes 28
  424.5 253.1 %all-reduce.5.cloned.1.call-start = ((), (), s32[]{:S(2)}) async-start(), calls=%async_computation.4 | async-start | bytes 524288 | tf_op jit(solution)/shard_map/psum | solution.py:115
  425.8 313.4 %reduce-scatter.5.cloned.1.call-start = ((), (), s32[]{:S(2)}) async-start(), calls=%async_computation.5 | async-start | bytes 2129920 | tf_op jit(solution)/shard_map/reduce_scatter | solution.py:143
  523.1 154.5 %copy-start = (f32[256,256]{0,1:T(8,128)S(1)}, f32[256,256]{0,1:T(8,128)}, u32[]{:S(2)}) copy-start(f32[256,256]{0,1:T(8,128)} %get-tuple-element.143) | copy-start | bytes 786436
Sparse Core Ops, SparseCore 0:
  12.2 80.7 all-gather.3
  121.9 159.1 reduce-scatter.2
  424.6 72.8 all-gather.5
  527.0 159.5 reduce-scatter.4
Sparse Core Ops, SparseCore 1:
  15.6 256.0 all-reduce.6
  431.3 246.2 all-reduce.4
where the time goes:
time: 837 us; the launch traced here: 827 us
  waiting for transfers between devices  448 us (54%)
  blocking collectives  155 us (19%)
  other arithmetic  133 us (16%)
  local copies, waits for them, and re-layouts  42.5 us (5%)
  between operations  19.3 us (2%)
  matrix products  17.4 us (2%)
  loops' own time  12.2 us (1%)
    psum x1, waiting for transfers between devices, body(): gram_a = lax.psum(local_a, ('ia', 'ja', 'ka'))  151 us
    psum x1, waiting for transfers between devices, body(): gram_b, gram_c = lax.psum((local_b, local_c), ('ia', 'ja', 'ka'))  150 us
    psum x1, blocking collectives, body(): squares_a = lax.psum(jnp.sum(a_hat * a_hat, axis=0), ('ia', 'ja', 'ka'))  77.9 us
    psum x1, blocking collectives, body(): squares_b = lax.psum(jnp.sum(b_hat * b_hat, axis=0), ('ia', 'ja', 'ka'))  77.3 us
    all_gather x1, waiting for transfers between devices, body(): lax.all_gather(factor_b.astype(jnp.bfloat16), ('ia', 'ka'), axis=1, tiled...  75.5 us
    all_gather x1, waiting for transfers between devices, body(): lax.all_gather(a_own.astype(jnp.bfloat16)[None], ('ja', 'ka'), axis=1, ti...  71.7 us
    another operation x13, other arithmetic, solve_rows(): lower = jnp.linalg.cholesky(gram)  68.6 us
    another operation x5, other arithmetic, solve_rows(): return jax.scipy.linalg.cho_solve((lower, True), rows.T).T  39.4 us
  transfers between devices with their start and end apart: 6, of which 4 were waited for; matrix products, arithmetic and copies ran while one was open for 22% of the time, Pallas kernels for 0%

commit v1 on v0

--- a/solution.py
+++ b/solution.py
@@ -112,7 +112,7 @@
     scale_a = jnp.sqrt(squares_a / total_one + EPS)
     a_own = a_hat / scale_a
     local_a = jnp.dot(a_own.T, a_own, precision=highest, preferred_element_type=jnp.float32)
-    gram_a = lax.psum(local_a, ("ia", "ja", "ka"))
+    gram_a = jnp.sum(lax.all_gather(local_a, ("ia", "ja", "ka")), axis=0)
     stored_a = lax.all_gather(a_own.astype(jnp.bfloat16)[None], ("ja", "ka"), axis=1, tiled=True)[0]
     half_a = to_logical(stored_a, owner_one, piece_rows)
 

time: 837 us -> 949 us (1.13)
  waiting for transfers between devices: 448 us -> 537 us
  other arithmetic: 133 us -> 153 us
    all_gather x0 -> x1, waiting for transfers between devices: none -> 185 us  [body(): gram_a = jnp.sum(lax.all_gather(local_a, ('ia', 'ja', 'ka')), axis=0)]
    psum x1 -> x0, waiting for transfers between devices: 151 us -> none  [body(): gram_a = lax.psum(local_a, ('ia', 'ja', 'ka'))]
    reduce_scatter x1, waiting for transfers between devices: 0.02 us -> 54.5 us  [body(): lax.psum_scatter(stored_two, ('ia', 'ka'), scatter_dimension=0, tiled=True)]
    reduce_sum x0 -> x1, other arithmetic: none -> 21.3 us  [body(): gram_a = jnp.sum(lax.all_gather(local_a, ('ia', 'ja', 'ka')), axis=0)]
  transfers between devices with their start and end apart: 6 -> 6, of which waited for: 4 -> 5; matrix products, arithmetic and copies ran while one was open for 22% -> 22% of each run, Pallas kernels for 0% -> 0%
where the time goes in v1:
time: 949 us; the launch traced here: 939 us
  waiting for transfers between devices  537 us (57%)
  blocking collectives  157 us (17%)
  other arithmetic  153 us (16%)
  local copies, waits for them, and re-layouts  42.9 us (5%)
  between operations  19.4 us (2%)
  matrix products  17.1 us (2%)
  loops' own time  11.8 us (1%)
    all_gather x1, waiting for transfers between devices, body(): gram_a = jnp.sum(lax.all_gather(local_a, ('ia', 'ja', 'ka')), axis=0)  185 us
    psum x1, waiting for transfers between devices, body(): gram_b, gram_c = lax.psum((local_b, local_c), ('ia', 'ja', 'ka'))  150 us
    psum x1, blocking collectives, body(): squares_b = lax.psum(jnp.sum(b_hat * b_hat, axis=0), ('ia', 'ja', 'ka'))  79.8 us
    psum x1, blocking collectives, body(): squares_a = lax.psum(jnp.sum(a_hat * a_hat, axis=0), ('ia', 'ja', 'ka'))  77.6 us
    all_gather x1, waiting for transfers between devices, body(): lax.all_gather(factor_b.astype(jnp.bfloat16), ('ia', 'ka'), axis=1, tiled...  75.5 us
    all_gather x1, waiting for transfers between devices, body(): lax.all_gather(a_own.astype(jnp.bfloat16)[None], ('ja', 'ka'), axis=1, ti...  72 us
    another operation x13, other arithmetic, solve_rows(): lower = jnp.linalg.cholesky(gram)  68.7 us
    reduce_scatter x1, waiting for transfers between devices, body(): lax.psum_scatter(stored_two, ('ia', 'ka'), scatter_dimension=0, tiled=True)  54.5 us
  transfers between devices with their start and end apart: 6, of which 5 were waited for; matrix products, arithmetic and copies ran while one was open for 22% of the time, Pallas kernels for 0%

profile of v1, /device:TPU:1, one launch (start us, length us, event | category | flops | bytes accessed | tf_op | source)
XLA Modules:
  0.0 939.4 jit_solution(7777731737193609385)
XLA Ops:
  9.5 2.0 fusion.34
  11.5 2.0 fusion.36
  17.5 75.5 %all-gather.6.cloned.1.call-done = bf16[1,2048,256]{2,1,0:T(8,128)(2,1)} async-done(((bf16[1,32,256]{2,1,0:T(8,128)(2,1)}), bf16[1,2048,256]{2,1,0:T(8,128)(2,1)}) %all-gather.6.cloned.1.call-update) | async-done | bytes 1048592 | tf_op jit(solution)/shard_map/all_gather | solution.py:80
  94.8 23.3 %conditional.4 = (f32[2048,256]{1,0:T(8,128)}) conditional(s32[]{:T(128)} %bitcast.41, () %tuple.54, (s32[1,1,1,2]{3,2,1,0:T(1,128)}, bf16[512,256]{1,0:T(8,128)(2,1)S(1)}, bf16[1,1,1,2,128,128,128]{6,5,4,3,2,1,0:T(8,128)(2,1)}, s32[1,1,1,2]{3,2,1,0:T(1,128)}, bf16[2048,256]{1,0:T(8,128)(2,1)S(1)}, /*index=5*/s32[1,1,1,2]{3,2,1,0:T(1,128)}) %tuple.134), branch_computations={%region_6.0_spmd, %region_7.0_spmd} | conditional | flops 1082130432 | bytes 83099928 | solution.py:104
  95.5 2.8 slice.76
  98.3 2.4 convolution_bitcast_fusion
  100.7 6.7 copy.55
  107.6 8.2 multiply_reduce_fusion
  118.1 3.6 gather_fusion.1
  122.1 149.5 %all-reduce.4.cloned.1.call-done = (f32[256,256]{0,1:T(8,128)}, f32[256,256]{0,1:T(8,128)}) async-done(((f32[256,256]{0,1:T(8,128)}, f32[256,256]{0,1:T(8,128)}), (f32[256,256]{0,1:T(8,128)}, f32[256,256]{0,1:T(8,128)})) %all-reduce.4.cloned.1.call-update) | async-done | bytes 524304 | tf_op jit(solution)/shard_map/psum | solution.py:79
  272.9 11.7 %cholesky.130 = f32[128,128]{1,0:T(8,128)S(1)} custom-call(f32[128,128]{1,0:T(8,128)S(1)} %cholesky.194), custom_call_target="Cholesky" | custom-call | tf_op jit(solution)/shard_map/jit(cholesky)/cholesky | solution.py:10
  284.6 9.8 %custom-call.15 = f32[1,128,128]{1,2,0:T(8,128)S(1)} custom-call(f32[1,128,128]{2,1,0:T(8,128)S(1)} %get-tuple-element.155), custom_call_target="InvertDiagBlocksLowerTriangular" | custom-call | tf_op jit(solution)/shard_map/jit(cholesky)/cholesky | solution.py:10
  295.0 11.7 %cholesky.147 = f32[128,128]{1,0:T(8,128)S(1)} custom-call(f32[128,128]{1,0:T(8,128)S(1)} %convolution_subtract_fusion.1), custom_call_target="Cholesky" | custom-call | tf_op jit(solution)/shard_map/jit(cholesky)/cholesky | solution.py:10
  308.9 14.6 %while.4 = (s32[]{:T(128)}, f32[256,256]{1,0:T(8,128)S(1)}, s32[2,2]{1,0:T(2,128)S(1)}, f32[2,128,128]{2,1,0:T(8,128)S(1)}, s32[]{:T(128)}) while((s32[]{:T(128)}, f32[256,256]{1,0:T(8,128)S(1)}, s32[2,2]{1,0:T(2,128)S(1)}, f32[2,128,128]{2,1,0:T(8,128)S(1)}, s32[]{:T(128)}) %tuple.103), condition=%wide.while_cond, body=%wide.while_body.sunk | while | flops 2 | bytes 131181 | solution.py:11
  323.5 19.7 %custom-call.16 = f32[2,128,128]{1,2,0:T(8,128)S(1)} custom-call(f32[2,128,128]{2,1,0:T(8,128)S(1)} %get-tuple-element.124), custom_call_target="InvertDiagBlocksLowerTriangular" | custom-call | tf_op jit(solution)/shard_map/jit(_cho_solve)/triangular_solve | solution.py:11
  345.8 77.6 %psum.30 = f32[256]{0:T(256)S(1)} all-reduce(f32[256]{0:T(256)S(1)} %multiply_reduce_fusion.5), channel_id=1, replica_groups=mesh['ia'=4,'ja'=4,'ka'=16] {'ia','ja','ka'}, use_global_device_ids=true, to_apply=%region_13.16 | all-reduce | flops 256 | bytes 2048 | tf_op jit(solution)/shard_map/psum | solution.py:111
  425.4 72.0 %all-gather.10.cloned.1.call-done = bf16[2048,256]{1,0:T(8,128)(2,1)} async-done(((bf16[32,256]{1,0:T(8,128)(2,1)}), bf16[2048,256]{1,0:T(8,128)(2,1)}) %all-gather.10.cloned.1.call-update) | async-done | bytes 1048592 | tf_op jit(solution)/shard_map/all_gather | solution.py:116
  499.2 23.7 %conditional.6 = (f32[2048,256]{1,0:T(8,128)}) conditional(s32[]{:T(128)} %bitcast.41, () %tuple.57, (s32[1,1,1,2]{3,2,1,0:T(1,128)S(1)}, bf16[2048,256]{1,0:T(8,128)(2,1)S(1)}, bf16[1,1,1,2,128,128,128]{6,5,4,3,2,1,0:T(8,128)(2,1)}, s32[1,1,1,2]{3,2,1,0:T(1,128)S(1)}, bf16[512,256]{1,0:T(8,128)(2,1)S(1)}, ...), branch_computations={%region_15.18_spmd, %region_16.19_spmd} | conditional | flops 1082130432 | bytes 83099800 | solution.py:139
  499.3 2.5 slice.84
  501.8 3.6 convolution_bitcast_fusion.2
  505.4 6.8 copy.58
  512.3 8.4 multiply_reduce_fusion.2
  523.2 3.6 gather_fusion.3
  526.8 185.1 %all-gather.8.cloned.1.call-done = f32[65536,256]{1,0:T(8,128)} async-done(((f32[256,256]{1,0:T(8,128)}), f32[65536,256]{1,0:T(8,128)}) %all-gather.8.cloned.1.call-update) | async-done | bytes 67108880 | tf_op jit(solution)/shard_map/all_gather | solution.py:115
  711.9 21.3 %reduce_sum.52 = f32[256,256]{1,0:T(8,128)S(1)} reduce(f32[256,256,256]{2,1,0:T(8,128)} %bitcast.52, f32[]{:T(128)} %constant.148.clone.1), dimensions={0}, to_apply=%region_14.17 | reduce | flops 16711680 | bytes 67371008 | tf_op jit(solution)/shard_map/reduce_sum | solution.py:115
  733.6 11.7 %cholesky.164 = f32[128,128]{1,0:T(8,128)S(1)} custom-call(f32[128,128]{1,0:T(8,128)S(1)} %cholesky.197), custom_call_target="Cholesky" | custom-call | tf_op jit(solution)/shard_map/jit(cholesky)/cholesky | solution.py:10
  745.4 9.8 %custom-call.17 = f32[1,128,128]{1,2,0:T(8,128)S(1)} custom-call(f32[1,128,128]{2,1,0:T(8,128)S(1)} %get-tuple-element.151), custom_call_target="InvertDiagBlocksLowerTriangular" | custom-call | tf_op jit(solution)/shard_map/jit(cholesky)/cholesky | solution.py:10
  755.7 11.7 %cholesky.181 = f32[128,128]{1,0:T(8,128)S(1)} custom-call(f32[128,128]{1,0:T(8,128)S(1)} %convolution_subtract_fusion), custom_call_target="Cholesky" | custom-call | tf_op jit(solution)/shard_map/jit(cholesky)/cholesky | solution.py:10
  770.1 4.1 while.5
  774.3 19.9 %custom-call.18 = f32[2,128,128]{1,2,0:T(8,128)S(1)} custom-call(f32[2,128,128]{2,1,0:T(8,128)S(1)} %get-tuple-element.125), custom_call_target="InvertDiagBlocksLowerTriangular" | custom-call | tf_op jit(solution)/shard_map/jit(_cho_solve)/triangular_solve | solution.py:11
  794.2 54.5 %reduce-scatter.5.cloned.1.call-done = f32[32,256]{1,0:T(8,128)} async-done(((f32[2048,256]{1,0:T(8,128)}), f32[32,256]{1,0:T(8,128)}) %reduce-scatter.5.cloned.1.call-update) | async-done | bytes 32784 | tf_op jit(solution)/shard_map/reduce_scatter | solution.py:143
  851.4 79.8 %psum.31 = f32[256]{0:T(256)S(1)} all-reduce(f32[256]{0:T(256)S(1)} %multiply_reduce_fusion.4), channel_id=1, replica_groups=mesh['ia'=4,'ja'=4,'ka'=16] {'ia','ja','ka'}, use_global_device_ids=true, to_apply=%region_22.25 | all-reduce | flops 256 | bytes 2048 | tf_op jit(solution)/shard_map/psum | solution.py:145
  (111 shorter events, 34.4 us)
Async XLA Ops:
  8.0 85.0 %all-gather.6.cloned.1.call-start = ((), (), s32[]{:S(2)}) async-start(), calls=%async_computation.2 | async-start | bytes 1064960 | tf_op jit(solution)/shard_map/all_gather | solution.py:80
  9.4 262.2 %all-reduce.4.cloned.1.call-start = ((), (), s32[]{:S(2)}) async-start(), calls=%async_computation.7 | async-start | bytes 1048576 | tf_op jit(solution)/shard_map/psum | solution.py:79
  13.4 329.7 %reduce-scatter.3.cloned.1.call-start = ((), (), s32[]{:S(2)}) async-start(), calls=%async_computation.3 | async-start | bytes 2129920 | tf_op jit(solution)/shard_map/reduce_scatter | solution.py:109
  100.7 6.7 copy-start.4
  107.5 8.4 copy-start.7
  121.7 303.6 %copy-start.1 = (s32[64]{0:T(128)S(1)}, s32[64]{0:T(128)}, u32[]{:S(2)}) copy-start(s32[64]{0:T(128)} %param.25) | copy-start | bytes 772
  121.8 377.5 %copy-start.2 = (s32[1,1,1,2]{3,2,1,0:T(1,128)S(1)}, s32[1,1,1,2]{3,2,1,0:T(1,128)}, u32[]{:S(2)}) copy-start(s32[1,1,1,2]{3,2,1,0:T(1,128)} %param.23) | copy-start | bytes 28
  121.8 377.4 %copy-start.3 = (s32[1,1,1,2]{3,2,1,0:T(1,128)S(1)}, s32[1,1,1,2]{3,2,1,0:T(1,128)}, u32[]{:S(2)}) copy-start(s32[1,1,1,2]{3,2,1,0:T(1,128)} %param.22) | copy-start | bytes 28
  121.8 377.4 %copy-start.6 = (s32[1,1,1,2]{3,2,1,0:T(1,128)S(1)}, s32[1,1,1,2]{3,2,1,0:T(1,128)}, u32[]{:S(2)}) copy-start(s32[1,1,1,2]{3,2,1,0:T(1,128)} %param.21) | copy-start | bytes 28
  121.8 375.6 %all-gather.10.cloned.1.call-start = ((), (), s32[]{:S(2)}) async-start(), calls=%async_computation.6 | async-start | bytes 1064960 | tf_op jit(solution)/shard_map/all_gather | solution.py:116
  424.1 287.8 %all-gather.8.cloned.1.call-start = ((), (), s32[]{:S(2)}) async-start(), calls=%async_computation.5 | async-start | bytes 67371008 | tf_op jit(solution)/shard_map/all_gather | solution.py:115
  425.3 423.4 %reduce-scatter.5.cloned.1.call-start = ((), (), s32[]{:S(2)}) async-start(), calls=%async_computation.4 | async-start | bytes 2129920 | tf_op jit(solution)/shard_map/reduce_scatter | solution.py:143
  711.9 21.4 %copy-start = (f32[256,256]{0,1:T(8,128)S(1)}, f32[256,256]{0,1:T(8,128)}, u32[]{:S(2)}) copy-start(f32[256,256]{0,1:T(8,128)} %get-tuple-element.143) | copy-start | bytes 786436
Sparse Core Ops, SparseCore 0:
  12.2 80.7 all-gather.5
  121.9 159.1 reduce-scatter.2
  424.2 73.0 all-gather.9
  501.6 210.3 all-gather.7
  716.4 132.3 reduce-scatter.4
Sparse Core Ops, SparseCore 1:
  15.6 256.0 all-reduce.3
